TPU v7x, 128 devices: a whole 4x4x4 slice. The times are simulated.
128 devices in a mesh: dp: 4 (over y_hi, core), mp: 32 (over x, z, y_lo).
Axes of the slice: x: 4, y: 4 (y_hi: 2, y_lo: 2; y = y_hi * 2 + y_lo), z: 4, core: 2. Of those that a mesh axis runs over, the one named last changes fastest.
Arguments:
- step_ids: int32 [32, 4], P('dp'), may hold values from 0 to 31999
- prompt_lens: int32 [32], P('dp'), may hold values from 128 to 1024
- embed_table: bfloat16 [32000, 4096], P(None, 'mp'), may hold values from -170 to 170
- attn_gain: bfloat16 [4096], replicated, may hold values from 0.099609375 to 1.8984375
- w_qkv: bfloat16 [3, 4096, 4096], P(None, None, 'mp'), may hold values from -0.09375 to 0.09375
- w_out: bfloat16 [4096, 4096], P('mp'), may hold values from -0.1875 to 0.1875
- key_cache: bfloat16 [32, 32, 1024, 128], P('dp', 'mp'), may hold values from -194 to 194
- value_cache: bfloat16 [32, 32, 1024, 128], P('dp', 'mp'), may hold values from -6 to 6
- reward_pieces: bfloat16 [32, 4096, 4096], P('dp', None, 'mp'), may hold values from -170 to 170
- piece_lens: int32 [32], P('dp'), may hold values from 256 to 4096
- reward_gain: bfloat16 [4096], replicated, may hold values from 0.099609375 to 1.8984375
- w_value: bfloat16 [4096, 2048], P('mp'), may hold values from -0.09375 to 0.09375
- b_value: float32 [2048], replicated, may hold values from -4 to 4
- w_score: float32 [2048], replicated, may hold values from -0.125 to 0.125
- b_score: float32 [1], replicated, may hold values from -3 to 3
Outputs:
- attn_out: bfloat16 [32, 4, 4096], P('dp')
- piece_values: float32 [32, 4096], P('dp', 'mp')
All inputs are finite; a program needn't handle non-finite values.
Results may differ from a plain program's by a relative error of at most 0.015.
Values may be sent and summed in bfloat16 or wider, within the bound.
No kernel may reach another device: no remote copies, remote signals or barrier semaphores. Data moves between devices by JAX's collectives and lax.ppermute only.
A program may use at most 192 MiB of HBM per device.

v0:
```python
import math

import jax
import jax.numpy as jnp
from jax import lax
from jax.sharding import PartitionSpec as P

epsilon = 1e-05
masked = -1e30


def normalize(rows_in, gain_vec):
    widened = rows_in.astype(jnp.float32)
    inverse_rms = lax.rsqrt(jnp.mean(widened * widened, axis=-1, keepdims=True) + epsilon)
    return (widened * inverse_rms * gain_vec.astype(jnp.float32)).astype(jnp.bfloat16)


def rotate(vectors, positions):
    half_dim = vectors.shape[-1] // 2
    frequency = 10000.0 ** (-2.0 * jnp.arange(half_dim, dtype=jnp.float32) / (2 * half_dim))
    angles = positions.astype(jnp.float32)[:, None, None] * frequency
    cosines = jnp.cos(angles)
    sines = jnp.sin(angles)
    first_half = vectors[..., :half_dim]
    second = vectors[..., half_dim:]
    return jnp.concatenate(
        [first_half * cosines - second * sines, second * cosines + first_half * sines], axis=-1
    )


def project(normed, w_qkv, positions, head_dim):
    projected = jnp.einsum("nd,cde->nce", normed, w_qkv, preferred_element_type=jnp.float32)
    head_count = projected.shape[2] // head_dim
    projected = projected.reshape(projected.shape[0], 3, head_count, head_dim)
    queries = rotate(projected[:, 0], positions).astype(jnp.bfloat16)
    new_key = rotate(projected[:, 1], positions).astype(jnp.bfloat16)
    new_value = projected[:, 2].astype(jnp.bfloat16)
    return (queries, new_key, new_value)


def attend(queries, key_cache, value_cache, live_slots, new_keys, new_values, query_steps):
    inverse_root = 1.0 / math.sqrt(queries.shape[-1])
    cache_scores = (
        jnp.einsum("rhqd,rhld->rhql", queries, key_cache, preferred_element_type=jnp.float32)
        * inverse_root
    )
    cache_scores = jnp.where(live_slots[:, None, None, :], cache_scores, masked)
    new_scores = (
        jnp.einsum("rhqd,rhsd->rhqs", queries, new_keys, preferred_element_type=jnp.float32)
        * inverse_root
    )
    causal = jnp.arange(new_keys.shape[2], dtype=jnp.int32)[None, :] <= query_steps[:, None]
    new_scores = jnp.where(causal[None, None], new_scores, masked)
    row_max = jnp.maximum(
        jnp.max(cache_scores, axis=-1, keepdims=True), jnp.max(new_scores, axis=-1, keepdims=True)
    )
    cache_weights = jnp.exp(cache_scores - row_max)
    new_weights = jnp.exp(new_scores - row_max)
    weight_total = jnp.sum(cache_weights, axis=-1) + jnp.sum(new_weights, axis=-1)
    mixed = jnp.einsum(
        "rhql,rhld->rhqd",
        cache_weights.astype(jnp.bfloat16),
        value_cache,
        preferred_element_type=jnp.float32,
    )
    mixed = mixed + jnp.einsum(
        "rhqs,rhsd->rhqd",
        new_weights.astype(jnp.bfloat16),
        new_values,
        preferred_element_type=jnp.float32,
    )
    return (mixed / weight_total[..., None]).astype(jnp.bfloat16)


def combine_heads(partial_sum):
    return lax.psum(partial_sum, "mp").astype(jnp.bfloat16)


def per_device(
    step_ids,
    prompt_lens,
    embed_table,
    attn_gain,
    w_qkv,
    w_out,
    key_cache,
    value_cache,
    reward_pieces,
    piece_lens,
    reward_gain,
    w_value,
    b_value,
    w_score,
    b_score,
):
    row_count, step_count = step_ids.shape
    head_dim = key_cache.shape[3]
    cache_slots = jnp.arange(key_cache.shape[2], dtype=jnp.int32)
    live_slots = cache_slots[None, :] < prompt_lens[:, None]
    key_list = []
    value_list = []
    results = []
    for step_index in range(step_count):
        local_rows = jnp.take(embed_table, step_ids[:, step_index], axis=0)
        full_rows = lax.all_gather(local_rows, "mp", axis=1, tiled=True)
        normed = normalize(full_rows, attn_gain)
        queries, new_key, new_value = project(normed, w_qkv, prompt_lens + step_index, head_dim)
        key_list.append(new_key[:, :, None, :])
        value_list.append(new_value[:, :, None, :])
        head_out = attend(
            queries[:, :, None, :],
            key_cache,
            value_cache,
            live_slots,
            jnp.concatenate(key_list, axis=2),
            jnp.concatenate(value_list, axis=2),
            jnp.array([step_index], dtype=jnp.int32),
        )
        partial_sum = jnp.dot(
            head_out.reshape(row_count, -1), w_out, preferred_element_type=jnp.float32
        )
        results.append(combine_heads(partial_sum[:, None, :]))
    attn_out = jnp.concatenate(results, axis=1)
    normed_pieces = normalize(
        lax.all_to_all(reward_pieces, "mp", split_axis=1, concat_axis=2, tiled=True), reward_gain
    )
    piece_count, seq_local, model_width = normed_pieces.shape
    token_rows = normed_pieces.reshape(piece_count * seq_local, model_width)
    preact = jnp.dot(
        token_rows,
        lax.all_gather(w_value, "mp", axis=0, tiled=True),
        preferred_element_type=jnp.float32,
    )
    hidden = jax.nn.silu(preact + b_value)
    scored = jnp.dot(hidden, w_score, precision=lax.Precision.HIGHEST) + b_score[0]
    scored = scored.reshape(piece_count, seq_local)
    positions_here = lax.axis_index("mp") * seq_local + jnp.arange(seq_local, dtype=jnp.int32)
    piece_values = jnp.where(positions_here[None, :] < piece_lens[:, None], scored, 0.0)
    return (attn_out, piece_values)


def solution(mesh):
    return jax.shard_map(
        per_device,
        mesh=mesh,
        in_specs=(
            P("dp", None),
            P("dp"),
            P(None, "mp"),
            P(),
            P(None, None, "mp"),
            P("mp", None),
            P("dp", "mp", None, None),
            P("dp", "mp", None, None),
            P("dp", None, "mp"),
            P("dp"),
            P(),
            P("mp", None),
            P(),
            P(),
            P(),
        ),
        out_specs=(P("dp", None, None), P("dp", "mp")),
        check_vma=False,
    )
```

profile of v0, /device:TPU:0, one launch (start us, length us, event | category | flops | bytes accessed | tf_op | source)
XLA Modules:
  0.0 725.0 jit_solution(3366700105728323592)
XLA Ops:
  7.2 0.7 all-gather.2.cloned.1.call-update
  7.9 10.5 %copy.97 = bf16[8,4096,128]{2,0,1:T(8,128)(2,1)} copy(bf16[8,4096,128]{2,1,0:T(8,128)(2,1)} %param.29) | data formatting | bytes 16777216 | tf_op args[8]
  18.5 9.6 %all-to-all-start = ((bf16[8,4096,128]{2,0,1:T(8,128)(2,1)}), bf16[8,4096,128]{2,0,1:T(8,128)(2,1)}, u32[]{:S(2)}, u32[]{:S(2)}) async-start(bf16[8,4096,128]{2,0,1:T(8,128)(2,1)} %copy.97), calls=%async_computation | async-start | bytes 16777216 | tf_op jit(solution)/shard_map/all_to_all | solution.py:125
  28.1 5.0 gather_fusion
  33.1 4.9 gather_fusion.3
  38.0 4.9 gather_fusion.2
  43.0 4.9 gather_fusion.1
  48.0 196.1 %all_gather.15 = bf16[8,4096]{1,0:T(8,128)(2,1)S(1)} all-gather(bf16[8,128]{1,0:T(8,128)(2,1)S(1)} %broadcast_select_fusion.3), channel_id=1, replica_groups=mesh['dp'=4,'mp'=32] {'mp'}, dimensions={1}, use_global_device_ids=true | all-gather | bytes 67584 | tf_op jit(solution)/shard_map/all_gather | solution.py:105
  244.2 76.6 %all_gather.18 = bf16[8,4096]{1,0:T(8,128)(2,1)S(1)} all-gather(bf16[8,128]{1,0:T(8,128)(2,1)S(1)} %broadcast_select_fusion), channel_id=1, replica_groups=mesh['dp'=4,'mp'=32] {'mp'}, dimensions={1}, use_global_device_ids=true | all-gather | bytes 67584 | tf_op jit(solution)/shard_map/all_gather | solution.py:105
  320.9 79.8 %all_gather.17 = bf16[8,4096]{1,0:T(8,128)(2,1)S(1)} all-gather(bf16[8,128]{1,0:T(8,128)(2,1)S(1)} %broadcast_select_fusion.1), channel_id=1, replica_groups=mesh['dp'=4,'mp'=32] {'mp'}, dimensions={1}, use_global_device_ids=true | all-gather | bytes 67584 | tf_op jit(solution)/shard_map/all_gather | solution.py:105
  400.7 77.0 %all_gather.16 = bf16[8,4096]{1,0:T(8,128)(2,1)S(1)} all-gather(bf16[8,128]{1,0:T(8,128)(2,1)S(1)} %broadcast_select_fusion.2), channel_id=1, replica_groups=mesh['dp'=4,'mp'=32] {'mp'}, dimensions={1}, use_global_device_ids=true | all-gather | bytes 67584 | tf_op jit(solution)/shard_map/all_gather | solution.py:105
  481.3 0.6 fusion.29
  482.7 0.6 slice.259
  483.8 0.6 fusion.23
  484.4 0.7 fusion.25
  485.1 0.7 fusion.27
  488.4 0.8 fusion.71
  491.1 1.9 fusion.197
  493.0 1.3 copy.132
  494.3 0.7 add.188
  494.9 0.7 slice_bitcast_fusion.9
  495.6 0.7 slice_bitcast_fusion.8
  496.3 0.7 maximum_bitcast_fusion.1
  497.0 0.8 fusion.85
  498.5 158.8 %all-reduce.2 = (bf16[8,1,4096]{2,0,1:T(8,128)(2,1)S(1)}, bf16[8,1,4096]{2,0,1:T(8,128)(2,1)S(1)}, bf16[8,1,4096]{2,0,1:T(8,128)(2,1)S(1)}, bf16[8,1,4096]{2,0,1:T(8,128)(2,1)S(1)}) all-reduce(f32[8,1,4096]{2,0,1:T(8,128)S(1)} %convolution_bitcast_fusion, ...), channel_id=1, replica_groups=mesh['dp'=4,'mp'=32] {'mp'}, use_global_device_ids=true, to_apply=%region_21.23 | all-reduce | flops 131072 | bytes 786432 | tf_op jit(solution)/shard_map/psum | solution.py:76
  657.3 0.9 copy.100
  658.2 0.7 convert_element_type.246
  659.6 13.9 %copy.98 = f32[8,32,128,128]{3,1,2,0:T(8,128)} copy(bf16[8,32,128,128]{3,0,2,1:T(8,128)(2,1)} %bitcast.258) | data formatting | bytes 25165824 | tf_op jit(solution)/shard_map/convert_element_type | solution.py:13
  673.5 8.5 %multiply_reduce_fusion = f32[8,4096]{0,1:T(8,128)S(1)} fusion(bf16[8,4096,128]{2,0,1:T(8,128)(2,1)} %all-to-all-done), kind=kLoop, calls=%fused_computation.7 | loop fusion | flops 12550144 | bytes 8519680 | tf_op jit(solution)/shard_map/reduce_sum | solution.py:14
  682.3 26.2 %fusion.2 = f32[1024,2048]{1,0:T(8,128)S(1)} fusion(bf16[4096,2048]{1,0:T(8,128)(2,1)} %all-gather.2.cloned.1.call-done, f32[128,8,32,128]{3,2,1,0:T(8,128)} %bitcast.281, f32[4096]{0:T(1024)S(1)} %convert_element_type.246, f32[1024]{0:T(1024)S(1)} %rsqrt_bitcast_fusion), kind=kOutput, calls=%fused_computation.8 | convolution fusion | flops 17192452096 | bytes 41963520 | tf_op jit(solution)/shard_map/dot_general | solution.py:129
  708.6 8.8 %fusion.4 = f32[1,1024]{1,0:T(1,128)S(1)} fusion(f32[2048,1]{0,1:T(1,128)S(1)} %bitcast.306, f32[1024,2048]{1,0:T(8,128)S(1)} %fusion.2, f32[2048]{0:T(1024)S(1)} %copy-done.15), kind=kOutput, calls=%fused_computation.9 | convolution fusion | flops 35651584 | bytes 8409088 | tf_op jit(solution)/shard_map/dot_general | solution.py:135
  717.4 0.7 bitcast_select_fusion
  (118 shorter events, 10.6 us)
Async XLA Ops:
  7.2 470.9 %copy-start = (bf16[3,4096,128]{2,1,0:T(8,128)(2,1)S(1)}, bf16[3,4096,128]{2,1,0:T(8,128)(2,1)}, u32[]{:S(2)}) copy-start(bf16[3,4096,128]{2,1,0:T(8,128)(2,1)} %param.25) | copy-start | bytes 9437188
  7.2 675.1 %all-gather.2.cloned.1.call-start = ((), (), s32[]{:S(2)}) async-start(), calls=%async_computation.1 | async-start | bytes 17301504 | tf_op jit(solution)/shard_map/all_gather | solution.py:131
  18.5 9.6 %copy-start.9 = (bf16[4096]{0:T(1024)(128)(2,1)S(1)}, bf16[4096]{0:T(1024)(128)(2,1)}, u32[]{:S(2)}) copy-start(bf16[4096]{0:T(1024)(128)(2,1)} %param.24) | copy-start | bytes 24580
  18.5 9.6 %copy-start.11 = (s32[8,4]{0,1:T(4,128)S(1)}, s32[8,4]{0,1:T(4,128)}, u32[]{:S(2)}) copy-start(s32[8,4]{0,1:T(4,128)} %param.21) | copy-start | bytes 388
  18.5 459.6 %copy-start.8 = (s32[8]{0:T(128)S(1)}, s32[8]{0:T(128)}, u32[]{:S(2)}) copy-start(s32[8]{0:T(128)} %param.22) | copy-start | bytes 100
  18.5 641.1 %all-to-all-start = ((bf16[8,4096,128]{2,0,1:T(8,128)(2,1)}), bf16[8,4096,128]{2,0,1:T(8,128)(2,1)}, u32[]{:S(2)}, u32[]{:S(2)}) async-start(bf16[8,4096,128]{2,0,1:T(8,128)(2,1)} %copy.97), calls=%async_computation | async-start | bytes 16777216 | tf_op jit(solution)/shard_map/all_to_all | solution.py:125
  479.7 1.6 copy-start.2
  480.3 3.5 copy-start.5
  480.8 2.9 copy-start.6
  483.7 2.2 copy-start.3
  484.4 2.0 copy-start.4
  487.3 1.2 copy-start.7
  487.8 0.5 copy-start.12
  488.3 0.9 copy-start.10
  682.3 26.3 %copy-start.14 = (f32[2048]{0:T(1024)S(1)}, f32[2048]{0:T(1024)}, u32[]{:S(2)}) copy-start(f32[2048]{0:T(1024)} %param.34) | copy-start | bytes 24580
  682.3 26.3 %copy-start.15 = (f32[2048]{0:T(1024)S(1)}, f32[2048]{0:T(1024)}, u32[]{:S(2)}) copy-start(f32[2048]{0:T(1024)} %param.33) | copy-start | bytes 24580
  708.6 8.9 %copy-start.13 = (s32[8]{0:T(128)S(1)}, s32[8]{0:T(128)}, u32[]{:S(2)}) copy-start(s32[8]{0:T(128)} %param.30) | copy-start | bytes 100
  708.6 9.5 %copy-start.1 = (bf16[3,4096,128]{2,1,0:T(8,128)(2,1)S(1)}, bf16[3,4096,128]{2,1,0:T(8,128)(2,1)}, u32[]{:S(2)}) copy-start(bf16[3,4096,128]{2,1,0:T(8,128)(2,1)} %param.25) | copy-start | bytes 9437188
Sparse Core Ops, SparseCore 0:
  9.6 472.2 all-gather.1
where the time goes:
time: 726 us; the launch traced here: 725 us
  blocking collectives  588 us (81%)
  local copies, waits for them, and re-layouts  50.6 us (7%)
  matrix products  44 us (6%)
  other arithmetic  16.8 us (2%)
  between operations  15 us (2%)
  starting transfers between devices  9.59 us (1%)
    all_gather x4, blocking collectives, per_device(): full_rows = lax.all_gather(local_rows, 'mp', axis=1, tiled=True)  429 us
    psum x1, blocking collectives, combine_heads(): return lax.psum(partial_sum, 'mp').astype(jnp.bfloat16)  159 us
    dot_general x1, matrix products, per_device(): jnp.dot(token_rows, lax.all_gather(w_value, 'mp', axis=0, tiled=True), pr...  26.2 us
    gather x4, local copies, waits for them, and re-layouts, per_device(): local_rows = jnp.take(embed_table, step_ids[:, step_index], axis=0)  19.8 us
  transfers between devices with their start and end apart: 2, of which 0 were waited for; matrix products, arithmetic and copies ran while one was open for 10% of the time, Pallas kernels for 0%

commit v1 on v0

v1 whole, which is shorter than its diff:
```python
import functools
import math

import jax
import jax.numpy as jnp
from jax import lax
from jax.experimental import pallas as pl
from jax.experimental.pallas import tpu as pltpu
from jax.sharding import Mesh, PartitionSpec as P

EPS = 1e-05
MASKED = -1e30
DP = ("yhi", "core")
MP = ("x", "z", "ylo")
GROUP = 32
LANES = 128
TILE = 256
COLS = 512


def vmem():
    return pl.BlockSpec(memory_space=pltpu.VMEM)


def hbm():
    return pl.BlockSpec(memory_space=pl.ANY)


def attention_kernel(emb_ref, gain_ref, wqkv_ref, cos_ref, sin_ref, lens_ref, key_ref, value_ref, out_ref, normed_ref):
    tokens = emb_ref.shape[1]
    width = GROUP * LANES
    rows = key_ref.shape[0]
    steps = tokens // rows
    squares = jnp.zeros((tokens, LANES), jnp.float32)
    for s in range(GROUP):
        part = emb_ref[s].astype(jnp.float32)
        squares = squares + part * part
    mean = jnp.sum(squares, axis=-1, keepdims=True) / width
    inverse_rms = lax.rsqrt(mean + EPS)
    for s in range(GROUP):
        part = emb_ref[s].astype(jnp.float32) * inverse_rms * gain_ref[s : s + 1, :]
        normed_ref[:, s * LANES : (s + 1) * LANES] = part.astype(jnp.bfloat16)
    normed = normed_ref[...]
    parts = [jnp.dot(normed, wqkv_ref[c], preferred_element_type=jnp.float32) for c in range(3)]
    cos, sin = cos_ref[...], sin_ref[...]
    half = LANES // 2

    def rotate(v):
        return (v * cos + pltpu.roll(v, half, 1) * sin).astype(jnp.bfloat16)

    queries, new_keys = rotate(parts[0]), rotate(parts[1])
    new_values = parts[2].astype(jnp.bfloat16)
    root = 1.0 / math.sqrt(LANES)
    slots = key_ref.shape[1]
    group_of = lax.broadcasted_iota(jnp.int32, (tokens, slots), 0) // steps
    scores = jnp.zeros((tokens, slots), jnp.float32)
    for r in range(rows):
        one = lax.dot_general(queries, key_ref[r], (((1,), (1,)), ((), ())), preferred_element_type=jnp.float32)
        scores = jnp.where(group_of == r, one, scores)
    live = lax.broadcasted_iota(jnp.int32, (tokens, slots), 1) < lens_ref[:, 0:1]
    scores = jnp.where(live, scores * root, MASKED)
    fresh = lax.dot_general(queries, new_keys, (((1,), (1,)), ((), ())), preferred_element_type=jnp.float32)
    i = lax.broadcasted_iota(jnp.int32, (tokens, tokens), 0)
    j = lax.broadcasted_iota(jnp.int32, (tokens, tokens), 1)
    causal = (i // steps == j // steps) & (j <= i)
    fresh = jnp.where(causal, fresh * root, MASKED)
    top = jnp.maximum(jnp.max(scores, axis=-1, keepdims=True), jnp.max(fresh, axis=-1, keepdims=True))
    weights = jnp.exp(scores - top)
    fresh_weights = jnp.exp(fresh - top)
    total = jnp.sum(weights, axis=-1, keepdims=True) + jnp.sum(fresh_weights, axis=-1, keepdims=True)
    mixed = jnp.dot(fresh_weights.astype(jnp.bfloat16), new_values, preferred_element_type=jnp.float32)
    for r in range(rows):
        own = jnp.where(group_of == r, weights, 0.0).astype(jnp.bfloat16)
        mixed = mixed + jnp.dot(own, value_ref[r], preferred_element_type=jnp.float32)
    out_ref[...] = (mixed / total).astype(jnp.bfloat16)


def attention(emb, gain, w_qkv, cos, sin, lens, keys, values):
    tokens = emb.shape[1]
    return pl.pallas_call(
        attention_kernel,
        out_shape=jax.ShapeDtypeStruct((tokens, LANES), jnp.bfloat16),
        in_specs=[vmem()] * 8,
        out_specs=vmem(),
        scratch_shapes=[pltpu.VMEM((tokens, GROUP * LANES), jnp.bfloat16)],
        compiler_params=pltpu.CompilerParams(vmem_limit_bytes=24 << 20),
        cost_estimate=pl.CostEstimate(flops=4 * 10**8, bytes_accessed=24 << 20, transcendentals=40000),
        name="attention",
    )(emb, gain, w_qkv, cos, sin, lens, keys, values)


def project_kernel(first, second, rows, w_ref, heads_ref, out_ref, w_buf, heads_buf, flat, sems):
    tokens = heads_buf.shape[1]
    w_copy = pltpu.make_async_copy(w_ref.at[:, pl.ds(first, rows), :], w_buf, sems.at[0])
    heads_copy = pltpu.make_async_copy(heads_ref.at[:, pl.ds(second, tokens), :], heads_buf, sems.at[1])
    w_copy.start()
    heads_copy.start()
    w_copy.wait()
    heads_copy.wait()
    for s in range(GROUP):
        flat[:, s * LANES : (s + 1) * LANES] = heads_buf[s]
    w = w_buf[...].reshape(GROUP * rows, LANES)
    out_ref[...] = jnp.dot(flat[...], w, preferred_element_type=jnp.float32).astype(jnp.bfloat16)


def project(w_message, w_row, heads_message, heads_row, tokens):
    return pl.pallas_call(
        functools.partial(project_kernel, w_row, heads_row, LANES),
        out_shape=jax.ShapeDtypeStruct((tokens, LANES), jnp.bfloat16),
        in_specs=[hbm(), hbm()],
        out_specs=vmem(),
        scratch_shapes=[
            pltpu.VMEM((GROUP, LANES, LANES), jnp.bfloat16),
            pltpu.VMEM((GROUP, tokens, LANES), jnp.bfloat16),
            pltpu.VMEM((tokens, GROUP * LANES), jnp.bfloat16),
            pltpu.SemaphoreType.DMA((2,)),
        ],
        compiler_params=pltpu.CompilerParams(vmem_limit_bytes=16 << 20),
        cost_estimate=pl.CostEstimate(flops=4 * 10**7, bytes_accessed=2 << 20, transcendentals=0),
        name="project",
    )(w_message, heads_message)


def score_kernel(tiles, x_hbm, wa_hbm, wb_hbm, gain_ref, bias_ref, score_ref, out_ref, x_buf, w_buf, normed_ref, x_sems, w_sems):
    width = GROUP * LANES
    span = width // 16

    def x_copy(t):
        return pltpu.make_async_copy(x_hbm.at[:, pl.ds(t * TILE, TILE), :], x_buf.at[t % 2], x_sems.at[t % 2])

    def w_copies(g):
        source = wa_hbm if g < 2 else wb_hbm
        return [
            pltpu.make_async_copy(source.at[k, g % 2], w_buf.at[g, pl.ds(k * span, span), :], w_sems.at[g])
            for k in range(16)
        ]

    x_copy(0).start()
    for g in range(4):
        for copy in w_copies(g):
            copy.start()
    for t in range(tiles):
        if t + 1 < tiles:
            x_copy(t + 1).start()
        x_copy(t).wait()
        squares = jnp.zeros((TILE, LANES), jnp.float32)
        for s in range(GROUP):
            part = x_buf[t % 2, s].astype(jnp.float32)
            squares = squares + part * part
        mean = jnp.sum(squares, axis=-1, keepdims=True) / width
        inverse_rms = lax.rsqrt(mean + EPS)
        for s in range(GROUP):
            part = x_buf[t % 2, s].astype(jnp.float32) * inverse_rms * gain_ref[s : s + 1, :]
            normed_ref[:, s * LANES : (s + 1) * LANES] = part.astype(jnp.bfloat16)
        total = jnp.zeros((TILE, LANES), jnp.float32)
        for g in range(4):
            if t == 0:
                pltpu.make_async_copy(w_buf.at[g], w_buf.at[g], w_sems.at[g]).wait()
            pre = jnp.dot(normed_ref[...], w_buf[g], preferred_element_type=jnp.float32)
            pre = pre + bias_ref[g : g + 1, :]
            hidden = pre / (1.0 + jnp.exp(-pre)) * score_ref[g : g + 1, :]
            for c in range(COLS // LANES):
                total = total + hidden[:, c * LANES : (c + 1) * LANES]
        out_ref[t : t + 1, :] = jnp.sum(total.T, axis=0, keepdims=True)


def score_rows(message, count, w_own, w_other, gain, bias, w_score):
    tiles = count // TILE
    width = GROUP * LANES
    return pl.pallas_call(
        functools.partial(score_kernel, tiles),
        out_shape=jax.ShapeDtypeStruct((tiles, TILE), jnp.float32),
        in_specs=[hbm(), hbm(), hbm(), vmem(), vmem(), vmem()],
        out_specs=vmem(),
        scratch_shapes=[
            pltpu.VMEM((2, GROUP, TILE, LANES), jnp.bfloat16),
            pltpu.VMEM((4, width, COLS), jnp.bfloat16),
            pltpu.VMEM((TILE, width), jnp.bfloat16),
            pltpu.SemaphoreType.DMA((2,)),
            pltpu.SemaphoreType.DMA((4,)),
        ],
        compiler_params=pltpu.CompilerParams(vmem_limit_bytes=40 << 20),
        cost_estimate=pl.CostEstimate(
            flops=2 * count * width * 4 * COLS, bytes_accessed=24 << 20, transcendentals=count * 4 * COLS
        ),
        name="score",
    )(message, w_own, w_other, gain, bias, w_score)


def exchange(message):
    return lax.all_to_all(message, MP, 0, 0)


def spread(block):
    return exchange(jnp.broadcast_to(block[None], (GROUP,) + block.shape))


def per_device(
    step_ids,
    prompt_lens,
    embed_table,
    attn_gain,
    w_qkv,
    w_out,
    key_cache,
    value_cache,
    reward_pieces,
    piece_lens,
    reward_gain,
    w_value,
    b_value,
    w_score,
    b_score,
):
    rows, steps = step_ids.shape
    tokens = rows * steps
    core = lax.axis_index("core")
    yhi = lax.axis_index("yhi")
    me = lax.axis_index(MP)

    quarter = lax.dynamic_slice_in_dim(w_value, (core * 2 + yhi) * COLS, COLS, axis=1)
    w_own = lax.all_gather(quarter[None], ("x", "z", "yhi", "ylo"), axis=0, tiled=True)
    w_own = w_own.reshape(16, 2, 2 * LANES, COLS)
    w_other = lax.ppermute(w_own, "core", [(0, 1), (1, 0)])
    order = jnp.stack([core, 1 - core])
    bias = b_value.reshape(2, 2, COLS)[order].reshape(4, COLS)
    score = w_score.reshape(2, 2, COLS)[order].reshape(4, COLS)

    local = embed_table.at[step_ids.reshape(tokens)].get(mode="promise_in_bounds")
    embedded = spread(local)
    half_dim = LANES // 2
    frequency = 10000.0 ** (-2.0 * jnp.arange(half_dim, dtype=jnp.float32) / (2 * half_dim))
    positions = (prompt_lens[:, None] + jnp.arange(steps, dtype=jnp.int32)[None, :]).reshape(tokens)
    angles = positions.astype(jnp.float32)[:, None] * frequency
    cos = jnp.concatenate([jnp.cos(angles)] * 2, axis=-1)
    sin = jnp.concatenate([-jnp.sin(angles), jnp.sin(angles)], axis=-1)
    lens = jnp.broadcast_to(jnp.repeat(prompt_lens, steps)[:, None], (tokens, LANES))
    heads = attention(
        embedded,
        attn_gain.astype(jnp.float32).reshape(GROUP, LANES),
        w_qkv,
        cos,
        sin,
        lens,
        key_cache.reshape(rows, -1, LANES),
        value_cache.reshape(rows, -1, LANES),
    )

    pieces, length, _ = reward_pieces.shape
    here = length // GROUP
    blocks = reward_pieces.reshape(pieces, GROUP, here, LANES).transpose(1, 0, 2, 3)
    split = pieces // 2
    count = split * here
    w_blocks = w_out.reshape(LANES, GROUP, LANES).transpose(1, 0, 2)
    first = exchange(jnp.concatenate([blocks[:, :split].reshape(GROUP, count, LANES), w_blocks], axis=1))
    second = exchange(
        jnp.concatenate(
            [
                blocks[:, split:].reshape(GROUP, count, LANES),
                jnp.broadcast_to(heads[None], (GROUP, tokens, LANES)),
            ],
            axis=1,
        )
    )
    gain = reward_gain.astype(jnp.float32).reshape(GROUP, LANES)
    scored = [score_rows(m, count, w_own, w_other, gain, bias, score) for m in (first, second)]
    scored = jnp.concatenate([s.reshape(split, here) for s in scored], axis=0) + b_score[0]
    where = me * here + jnp.arange(here, dtype=jnp.int32)
    piece_values = jnp.where(where[None, :] < piece_lens[:, None], scored, 0.0)

    columns = project(first, count, second, count, tokens)
    attn_out = spread(columns).transpose(1, 0, 2).reshape(rows, steps, GROUP * LANES)
    return (attn_out, piece_values)


def solution(mesh):
    fine = Mesh(mesh.devices.reshape(2, 2, 4, 4, 2), DP + MP)
    return jax.shard_map(
        per_device,
        mesh=fine,
        in_specs=(
            P(DP, None),
            P(DP),
            P(None, MP),
            P(),
            P(None, None, MP),
            P(MP, None),
            P(DP, MP, None, None),
            P(DP, MP, None, None),
            P(DP, None, MP),
            P(DP),
            P(),
            P(MP, None),
            P(),
            P(),
            P(),
        ),
        out_specs=(P(DP, None, None), P(DP, MP)),
        check_vma=False,
    )
```

time: 726 us -> 293 us (0.40)
  blocking collectives: 588 us -> 0 us
  waiting for transfers between devices: 0.69 us -> 163 us
  matrix products: 44 us -> 0 us
  Pallas kernels: 0 us -> 30.4 us
  starting transfers between devices: 9.59 us -> 35.1 us
  local copies, waits for them, and re-layouts: 50.6 us -> 40.2 us
  other arithmetic: 16.8 us -> 8.49 us
    all_gather x4 -> x0, blocking collectives: 429 us -> none  [per_device(): full_rows = lax.all_gather(local_rows, 'mp', axis=1, tiled=True)]
    psum x1 -> x0, blocking collectives: 159 us -> none  [combine_heads(): return lax.psum(partial_sum, 'mp').astype(jnp.bfloat16)]
    all_to_all x1 -> x4, waiting for transfers between devices: 0.01 us -> 87.6 us  [exchange(): return lax.all_to_all(message, MP, 0, 0)]
    all_gather x1, waiting for transfers between devices: 0.01 us -> 75.1 us  [per_device(): lax.all_gather(quarter[None], ('x', 'z', 'yhi', 'ylo'), axis=0, tiled=True)]
    dot_general x24 -> x0, matrix products: 44 us -> none  [the longest x1 26.2 us: per_device(): jnp.dot(token_rows, lax.all_gather(w_value, 'mp', axis=0, tiled=True), pr...]
    pallas_call x0 -> x4, Pallas kernels: none -> 30.4 us  [the longest x2 27 us: score_rows(): pl.pallas_call(functools.partial(score_kernel, tiles), out_shape=jax.Shap...]
    all_to_all x1 -> x4, starting transfers between devices: 9.55 us -> 35.1 us  [exchange(): return lax.all_to_all(message, MP, 0, 0)]
    convert_element_type x4 -> x0, local copies, waits for them, and re-layouts: 15.4 us -> none  [the longest x1 13.9 us: normalize(): widened = rows_in.astype(jnp.float32)]
  transfers between devices with their start and end apart: 2 -> 6, of which waited for: 0 -> 3; matrix products, arithmetic and copies ran while one was open for 10% -> 12% of each run, Pallas kernels for 0% -> 1%
where the time goes in v1:
time: 293 us; the launch traced here: 292 us
  waiting for transfers between devices  163 us (56%)
  local copies, waits for them, and re-layouts  40.2 us (14%)
  starting transfers between devices  35.1 us (12%)
  Pallas kernels  30.4 us (10%)
  between operations  14.9 us (5%)
  other arithmetic  8.49 us (3%)
    all_to_all x4, waiting for transfers between devices, exchange(): return lax.all_to_all(message, MP, 0, 0)  87.6 us
    all_gather x1, waiting for transfers between devices, per_device(): lax.all_gather(quarter[None], ('x', 'z', 'yhi', 'ylo'), axis=0, tiled=True)  75.1 us
    all_to_all x4, starting transfers between devices, exchange(): return lax.all_to_all(message, MP, 0, 0)  35.1 us
    pallas_call x2, Pallas kernels, score_rows(): pl.pallas_call(functools.partial(score_kernel, tiles), out_shape=jax.Shap...  27 us
    unnamed x30, local copies, waits for them, and re-layouts  12.6 us
    reshape x1, local copies, waits for them, and re-layouts, per_device(): reward_pieces.reshape(pieces, GROUP, here, LANES).transpose(1, 0, 2, 3)  10.4 us
    slice x1, local copies, waits for them, and re-layouts, per_device(): blocks[:, split:].reshape(GROUP, count, LANES)  6.26 us
  transfers between devices with their start and end apart: 6, of which 3 were waited for; matrix products, arithmetic and copies ran while one was open for 12% of the time, Pallas kernels for 1%

profile of v1, /device:TPU:0, one launch (start us, length us, event | category | flops | bytes accessed | tf_op | source)
XLA Modules:
  0.0 291.9 jit_solution(6494449751199176102)
XLA Ops:
  7.2 1.0 copy-done
  8.2 0.7 constant_dynamic-slice_fusion
  8.9 0.8 copy.30
  9.8 5.0 %gather_fusion = bf16[32,128]{1,0:T(8,128)(2,1)S(1)} fusion(bf16[32000,128]{1,0:T(8,128)(2,1)} %param.17, s32[1024]{0:T(1024)S(1)} %pad_clamp_fusion.1), kind=kCustom, calls=%fused_computation | custom fusion | bytes 16512 | tf_op jit(solution)/shard_map/gather | solution.py:229
  14.7 0.7 broadcast_in_dim.13
  15.5 9.3 %all-to-all-start.1 = ((bf16[32,32,128]{2,1,0:T(8,128)(2,1)}), bf16[32,32,128]{2,1,0:T(8,128)(2,1)S(1)}, u32[]{:S(2)}, u32[]{:S(2)}) async-start(bf16[32,32,128]{2,1,0:T(8,128)(2,1)} %broadcast_in_dim.13), calls=%async_computation.1 | async-start | bytes 524288 | tf_op jit(solution)/shard_map/all_to_all | solution.py:191
  24.8 0.7 add.76
  25.7 10.4 %copy.33 = bf16[8,32,128,128]{3,2,0,1:T(8,128)(2,1)} copy(bf16[8,32,128,128]{3,2,1,0:T(8,128)(2,1)} %bitcast.34) | data formatting | bytes 16777216 | tf_op jit(solution)/shard_map/reshape | solution.py:251
  36.2 6.3 %fusion.4 = (bf16[32,4,128,128]{3,2,1,0:T(8,128)(2,1)}, bf16[32,4,128,128]{3,2,1,0:T(8,128)(2,1)}) fusion(bf16[32,8,128,128]{3,2,1,0:T(8,128)(2,1)} %bitcast.31), kind=kLoop, calls=%fused_computation.25 | loop fusion | bytes 16777216 | tf_op jit(solution)/shard_map/slice | solution.py:259
  42.7 1.6 copy-done.3
  44.3 1.6 copy-done.4
  45.9 1.9 attention.1
  48.0 2.5 pad_maximum_fusion.1
  50.5 8.6 %all-to-all-start.2 = ((bf16[32,544,128]{2,1,0:T(8,128)(2,1)}), bf16[32,544,128]{2,1,0:T(8,128)(2,1)}, u32[]{:S(2)}, u32[]{:S(2)}) async-start(bf16[32,544,128]{2,1,0:T(8,128)(2,1)} %pad_maximum_fusion.1), calls=%async_computation.2 | async-start | bytes 8912896 | tf_op jit(solution)/shard_map/all_to_all | solution.py:191
  59.1 75.1 %all-gather.3.cloned.1.call-done = bf16[8192,512]{1,0:T(8,128)(2,1)} async-done(((bf16[128,512]{1,0:T(8,128)(2,1)}), bf16[8192,512]{1,0:T(8,128)(2,1)}) %all-gather.3.cloned.1.call-update) | async-done | bytes 8388624 | tf_op jit(solution)/shard_map/all_gather | solution.py:222
  134.2 0.7 copy.28
  134.8 0.7 copy.29
  135.5 5.0 %pad_maximum_fusion = bf16[32,640,128]{2,1,0:T(8,128)(2,1)} fusion(bf16[32,128,128]{2,1,0:T(8,128)(2,1)S(1)} %bitcast.35, bf16[32,512,128]{2,1,0:T(8,128)(2,1)} %bitcast.32), kind=kLoop, calls=%fused_computation.4 | loop fusion | flops 10485760 | bytes 10485760 | tf_op jit(solution)/shard_map/concatenate | solution.py:255
  140.5 10.2 %all-to-all-start = ((bf16[32,640,128]{2,1,0:T(8,128)(2,1)}), bf16[32,640,128]{2,1,0:T(8,128)(2,1)}, u32[]{:S(2)}, u32[]{:S(2)}) async-start(bf16[32,640,128]{2,1,0:T(8,128)(2,1)} %pad_maximum_fusion), calls=%async_computation | async-start | bytes 10485760 | tf_op jit(solution)/shard_map/all_to_all | solution.py:191
  150.8 80.5 %all-to-all-done.w_ref.x_hbm = bf16[32,640,128]{2,1,0:T(8,128)(2,1)} async-done(((bf16[32,640,128]{2,1,0:T(8,128)(2,1)}), bf16[32,640,128]{2,1,0:T(8,128)(2,1)}, u32[]{:S(2)}, u32[]{:S(2)}) %all-to-all-start) | async-done | bytes 5242912 | tf_op jit(solution)/shard_map/all_to_all | solution.py:191
  231.3 1.6 project.1
  232.9 0.7 broadcast_in_dim.16
  233.7 7.1 %all-to-all-start.3 = ((bf16[32,32,128]{2,1,0:T(8,128)(2,1)}), bf16[32,32,128]{2,1,0:T(8,128)(2,1)S(1)}, u32[]{:S(2)}, u32[]{:S(2)}) async-start(bf16[32,32,128]{2,1,0:T(8,128)(2,1)} %broadcast_in_dim.16), calls=%async_computation.3 | async-start | bytes 524288 | tf_op jit(solution)/shard_map/all_to_all | solution.py:191
  241.4 0.6 gather_fusion.1
  242.0 0.6 gather_fusion.2
  242.6 7.1 %all-to-all-done.3 = bf16[32,32,128]{2,1,0:T(8,128)(2,1)S(1)} async-done(((bf16[32,32,128]{2,1,0:T(8,128)(2,1)}), bf16[32,32,128]{2,1,0:T(8,128)(2,1)S(1)}, u32[]{:S(2)}, u32[]{:S(2)}) %all-to-all-start.3) | async-done | bytes 262176 | tf_op jit(solution)/shard_map/all_to_all | solution.py:191
  249.8 0.8 reshape.209
  250.6 3.4 %copy-done.5 = bf16[8192,512]{1,0:T(8,128)(2,1)S(1)} copy-done((bf16[8192,512]{1,0:T(8,128)(2,1)S(1)}, bf16[8192,512]{1,0:T(8,128)(2,1)}, u32[]{:S(2)}) %copy-start.5) | copy-done | bytes 8388632
  254.0 13.5 %score.3 = f32[2,256]{1,0:T(2,128)S(1)} custom-call(bf16[32,544,128]{2,1,0:T(8,128)(2,1)} %all-to-all-done.2.heads_ref.x_hbm, bf16[16,2,256,512]{3,2,1,0:T(8,128)(2,1)S(1)} %bitcast.29, bf16[16,2,256,512]{3,2,1,0:T(8,128)(2,1)} %collective-permute-done.wb_hbm, f32[32,128]{1,0:T(8,128)S(1)} %bitcast_convert_fusion.1.gain_ref, ...), custom_call_target="tpu_custom_call" | custom-call | flops 8589934592 | bytes 25165824 | tf_op jit(solution)/shard_map/score/pallas_call | solution.py:170
  267.5 3.4 %copy-done.6 = bf16[8192,512]{1,0:T(8,128)(2,1)S(1)} copy-done((bf16[8192,512]{1,0:T(8,128)(2,1)S(1)}, bf16[8192,512]{1,0:T(8,128)(2,1)}, u32[]{:S(2)}) %copy-start.6) | copy-done | bytes 8388632
  270.8 13.5 %score.2 = f32[2,256]{1,0:T(2,128)S(1)} custom-call(bf16[32,640,128]{2,1,0:T(8,128)(2,1)} %all-to-all-done.w_ref.x_hbm, bf16[16,2,256,512]{3,2,1,0:T(8,128)(2,1)S(1)} %bitcast.30, bf16[16,2,256,512]{3,2,1,0:T(8,128)(2,1)} %collective-permute-done.wb_hbm, f32[32,128]{1,0:T(8,128)S(1)} %bitcast_convert_fusion.1.gain_ref, f32[4,512]{1,0:T(4,128)S(1)} %reshape.214.bias_ref, ...), custom_call_target="tpu_custom_call" | custom-call | flops 8589934592 | bytes 25165824 | tf_op jit(solution)/shard_map/score/pallas_call | solution.py:170
  284.4 0.7 fusion.1
  (53 shorter events, 1.3 us)
Async XLA Ops:
  7.2 1.1 copy-start
  7.2 127.0 %all-gather.3.cloned.1.call-start = ((), (), s32[]{:S(2)}) async-start(), calls=%async_computation.4 | async-start | bytes 8519680 | tf_op jit(solution)/shard_map/all_gather | solution.py:222
  15.5 27.1 %all-to-all-start.1 = ((bf16[32,32,128]{2,1,0:T(8,128)(2,1)}), bf16[32,32,128]{2,1,0:T(8,128)(2,1)S(1)}, u32[]{:S(2)}, u32[]{:S(2)}) async-start(bf16[32,32,128]{2,1,0:T(8,128)(2,1)} %broadcast_in_dim.13), calls=%async_computation.1 | async-start | bytes 524288 | tf_op jit(solution)/shard_map/all_to_all | solution.py:191
  36.2 6.4 %copy-start.9 = (bf16[4096]{0:T(1024)(128)(2,1)S(1)}, bf16[4096]{0:T(1024)(128)(2,1)}, u32[]{:S(2)}) copy-start(bf16[4096]{0:T(1024)(128)(2,1)} %param.18) | copy-start | bytes 24580
  36.2 6.4 %copy-start.2 = (bf16[3,4096,128]{2,1,0:T(8,128)(2,1)S(1)}, bf16[3,4096,128]{2,1,0:T(8,128)(2,1)}, u32[]{:S(2)}) copy-start(bf16[3,4096,128]{2,1,0:T(8,128)(2,1)} %wqkv_ref.1) | copy-start | bytes 9437188
  42.7 1.6 copy-start.3
  44.3 1.6 copy-start.4
  45.9 2.2 copy-start.7
  50.5 83.7 %copy-start.8 = (bf16[128,4096]{1,0:T(8,128)(2,1)S(1)}, bf16[128,4096]{1,0:T(8,128)(2,1)}, u32[]{:S(2)}) copy-start(bf16[128,4096]{1,0:T(8,128)(2,1)} %param.20) | copy-start | bytes 3145732
  50.5 90.0 %all-to-all-start.2 = ((bf16[32,544,128]{2,1,0:T(8,128)(2,1)}), bf16[32,544,128]{2,1,0:T(8,128)(2,1)}, u32[]{:S(2)}, u32[]{:S(2)}) async-start(bf16[32,544,128]{2,1,0:T(8,128)(2,1)} %pad_maximum_fusion.1), calls=%async_computation.2 | async-start | bytes 8912896 | tf_op jit(solution)/shard_map/all_to_all | solution.py:191
  134.2 116.4 %collective-permute-start = (bf16[16,2,256,512]{3,2,1,0:T(8,128)(2,1)}, bf16[16,2,256,512]{3,2,1,0:T(8,128)(2,1)}, u32[]{:S(2)}, u32[]{:S(2)}) collective-permute-start(bf16[16,2,256,512]{3,2,1,0:T(8,128)(2,1)} %bitcast.28), channel_id=1, source_target_pairs={{0,32},{32,0},{1,33},{33,1},{2,34},{34,2},{3,35},{35,3},{4,36},{36... | collective-permute-start | bytes 25165832 | tf_op jit(solution)/shard_map/ppermute | solution.py:224
  140.5 90.8 %all-to-all-start = ((bf16[32,640,128]{2,1,0:T(8,128)(2,1)}), bf16[32,640,128]{2,1,0:T(8,128)(2,1)}, u32[]{:S(2)}, u32[]{:S(2)}) async-start(bf16[32,640,128]{2,1,0:T(8,128)(2,1)} %pad_maximum_fusion), calls=%async_computation | async-start | bytes 10485760 | tf_op jit(solution)/shard_map/all_to_all | solution.py:191
  150.8 90.6 %copy-start.11 = (f32[2048]{0:T(1024)S(1)}, f32[2048]{0:T(1024)}, u32[]{:S(2)}) copy-start(f32[2048]{0:T(1024)} %param.27) | copy-start | bytes 24580
  150.8 91.2 %copy-start.12 = (f32[2048]{0:T(1024)S(1)}, f32[2048]{0:T(1024)}, u32[]{:S(2)}) copy-start(f32[2048]{0:T(1024)} %param.28) | copy-start | bytes 24580
  150.8 91.8 %copy-start.10 = (bf16[4096]{0:T(1024)(128)(2,1)S(1)}, bf16[4096]{0:T(1024)(128)(2,1)}, u32[]{:S(2)}) copy-start(bf16[4096]{0:T(1024)(128)(2,1)} %param.25) | copy-start | bytes 24580
  233.7 16.0 %all-to-all-start.3 = ((bf16[32,32,128]{2,1,0:T(8,128)(2,1)}), bf16[32,32,128]{2,1,0:T(8,128)(2,1)S(1)}, u32[]{:S(2)}, u32[]{:S(2)}) async-start(bf16[32,32,128]{2,1,0:T(8,128)(2,1)} %broadcast_in_dim.16), calls=%async_computation.3 | async-start | bytes 524288 | tf_op jit(solution)/shard_map/all_to_all | solution.py:191
  250.6 3.4 %copy-start.5 = (bf16[8192,512]{1,0:T(8,128)(2,1)S(1)}, bf16[8192,512]{1,0:T(8,128)(2,1)}, u32[]{:S(2)}) copy-start(bf16[8192,512]{1,0:T(8,128)(2,1)} %all-gather.3.cloned.1.call-done) | copy-start | bytes 25165828
  267.4 3.4 %copy-start.6 = (bf16[8192,512]{1,0:T(8,128)(2,1)S(1)}, bf16[8192,512]{1,0:T(8,128)(2,1)}, u32[]{:S(2)}) copy-start(bf16[8192,512]{1,0:T(8,128)(2,1)} %all-gather.3.cloned.1.call-done) | copy-start | bytes 25165828
  270.8 13.5 %copy-start.13 = (s32[8]{0:T(128)S(1)}, s32[8]{0:T(128)}, u32[]{:S(2)}) copy-start(s32[8]{0:T(128)} %param.24) | copy-start | bytes 100
  270.8 14.2 %copy-start.1 = (bf16[128,2048]{1,0:T(8,128)(2,1)S(1)}, bf16[128,2048]{1,0:T(8,128)(2,1)}, u32[]{:S(2)}) copy-start(bf16[128,2048]{1,0:T(8,128)(2,1)} %param.26) | copy-start | bytes 1572868
Sparse Core Ops, SparseCore 0:
  10.9 123.2 all-gather.2

commit v2 on v1

--- a/solution.py
+++ b/solution.py
@@ -14,7 +14,6 @@
 MP = ("x", "z", "ylo")
 GROUP = 32
 LANES = 128
-TILE = 256
 COLS = 512
 
 
@@ -100,13 +99,14 @@
     for s in range(GROUP):
         flat[:, s * LANES : (s + 1) * LANES] = heads_buf[s]
     w = w_buf[...].reshape(GROUP * rows, LANES)
-    out_ref[...] = jnp.dot(flat[...], w, preferred_element_type=jnp.float32).astype(jnp.bfloat16)
+    columns = jnp.dot(flat[...], w, preferred_element_type=jnp.float32).astype(jnp.bfloat16)
+    out_ref[...] = columns.astype(jnp.float32)
 
 
 def project(w_message, w_row, heads_message, heads_row, tokens):
     return pl.pallas_call(
         functools.partial(project_kernel, w_row, heads_row, LANES),
-        out_shape=jax.ShapeDtypeStruct((tokens, LANES), jnp.bfloat16),
+        out_shape=jax.ShapeDtypeStruct((tokens, LANES), jnp.float32),
         in_specs=[hbm(), hbm()],
         out_specs=vmem(),
         scratch_shapes=[
@@ -121,70 +121,163 @@
     )(w_message, heads_message)
 
 
-def score_kernel(tiles, x_hbm, wa_hbm, wb_hbm, gain_ref, bias_ref, score_ref, out_ref, x_buf, w_buf, normed_ref, x_sems, w_sems):
+def score_kernel(slots, x_hbm, wa_hbm, wb_hbm, gain_ref, bias_ref, score_ref, out_ref, x_buf, w_buf, normed_ref, total_ref, x_sem, w_sems):
     width = GROUP * LANES
     span = width // 16
-
-    def x_copy(t):
-        return pltpu.make_async_copy(x_hbm.at[:, pl.ds(t * TILE, TILE), :], x_buf.at[t % 2], x_sems.at[t % 2])
-
-    def w_copies(g):
+    rows = slots * LANES
+    x_copy = pltpu.make_async_copy(x_hbm.at[:, pl.ds(0, rows), :], x_buf, x_sem.at[0])
+    x_copy.start()
+    for g in range(4):
         source = wa_hbm if g < 2 else wb_hbm
-        return [
-            pltpu.make_async_copy(source.at[k, g % 2], w_buf.at[g, pl.ds(k * span, span), :], w_sems.at[g])
-            for k in range(16)
-        ]
-
-    x_copy(0).start()
-    for g in range(4):
-        for copy in w_copies(g):
-            copy.start()
-    for t in range(tiles):
-        if t + 1 < tiles:
-            x_copy(t + 1).start()
-        x_copy(t).wait()
-        squares = jnp.zeros((TILE, LANES), jnp.float32)
+        for k in range(16):
+            pltpu.make_async_copy(source.at[k, g % 2], w_buf.at[g, pl.ds(k * span, span), :], w_sems.at[g]).start()
+    x_copy.wait()
+
+    @pl.loop(0, slots)
+    def _(q):
+        here = pl.ds(pl.multiple_of(q * LANES, LANES), LANES)
+        squares = jnp.zeros((LANES, LANES), jnp.float32)
         for s in range(GROUP):
-            part = x_buf[t % 2, s].astype(jnp.float32)
+            part = x_buf[s, here, :].astype(jnp.float32)
             squares = squares + part * part
         mean = jnp.sum(squares, axis=-1, keepdims=True) / width
         inverse_rms = lax.rsqrt(mean + EPS)
         for s in range(GROUP):
-            part = x_buf[t % 2, s].astype(jnp.float32) * inverse_rms * gain_ref[s : s + 1, :]
-            normed_ref[:, s * LANES : (s + 1) * LANES] = part.astype(jnp.bfloat16)
-        total = jnp.zeros((TILE, LANES), jnp.float32)
-        for g in range(4):
-            if t == 0:
-                pltpu.make_async_copy(w_buf.at[g], w_buf.at[g], w_sems.at[g]).wait()
-            pre = jnp.dot(normed_ref[...], w_buf[g], preferred_element_type=jnp.float32)
-            pre = pre + bias_ref[g : g + 1, :]
-            hidden = pre / (1.0 + jnp.exp(-pre)) * score_ref[g : g + 1, :]
-            for c in range(COLS // LANES):
-                total = total + hidden[:, c * LANES : (c + 1) * LANES]
-        out_ref[t : t + 1, :] = jnp.sum(total.T, axis=0, keepdims=True)
-
-
-def score_rows(message, count, w_own, w_other, gain, bias, w_score):
-    tiles = count // TILE
+            part = x_buf[s, here, :].astype(jnp.float32) * inverse_rms * gain_ref[s : s + 1, :]
+            normed_ref[here, s * LANES : (s + 1) * LANES] = part.astype(jnp.bfloat16)
+
+    total_ref[...] = jnp.zeros_like(total_ref)
+
+    @pl.loop(0, 4)
+    def _(g):
+        pltpu.make_async_copy(w_buf.at[g], w_buf.at[g], w_sems.at[g]).wait()
+        pre = jnp.dot(normed_ref[...], w_buf[g], preferred_element_type=jnp.float32)
+        pre = pre + bias_ref[pl.ds(g, 1), :]
+        hidden = pre / (1.0 + jnp.exp(-pre)) * score_ref[pl.ds(g, 1), :]
+        total = total_ref[...]
+        for c in range(COLS // LANES):
+            total = total + hidden[:, c * LANES : (c + 1) * LANES]
+        total_ref[...] = total
+
+    for q in range(slots):
+        out_ref[q : q + 1, :] = jnp.sum(total_ref[q * LANES : (q + 1) * LANES, :].T, axis=0, keepdims=True)
+
+
+def score_rows(message, slots, w_own, w_other, gain, bias, w_score):
     width = GROUP * LANES
+    rows = slots * LANES
     return pl.pallas_call(
-        functools.partial(score_kernel, tiles),
-        out_shape=jax.ShapeDtypeStruct((tiles, TILE), jnp.float32),
+        functools.partial(score_kernel, slots),
+        out_shape=jax.ShapeDtypeStruct((slots, LANES), jnp.float32),
         in_specs=[hbm(), hbm(), hbm(), vmem(), vmem(), vmem()],
         out_specs=vmem(),
         scratch_shapes=[
-            pltpu.VMEM((2, GROUP, TILE, LANES), jnp.bfloat16),
+            pltpu.VMEM((GROUP, rows, LANES), jnp.bfloat16),
             pltpu.VMEM((4, width, COLS), jnp.bfloat16),
-            pltpu.VMEM((TILE, width), jnp.bfloat16),
-            pltpu.SemaphoreType.DMA((2,)),
+            pltpu.VMEM((rows, width), jnp.bfloat16),
+            pltpu.VMEM((rows, LANES), jnp.float32),
+            pltpu.SemaphoreType.DMA((1,)),
             pltpu.SemaphoreType.DMA((4,)),
         ],
-        compiler_params=pltpu.CompilerParams(vmem_limit_bytes=40 << 20),
+        compiler_params=pltpu.CompilerParams(vmem_limit_bytes=56 << 20),
         cost_estimate=pl.CostEstimate(
-            flops=2 * count * width * 4 * COLS, bytes_accessed=24 << 20, transcendentals=count * 4 * COLS
+            flops=2 * rows * width * 4 * COLS, bytes_accessed=24 << 20, transcendentals=rows * 4 * COLS
         ),
         name="score",
     )(message, w_own, w_other, gain, bias, w_score)
+
+
+def block_starts(lens_ref, pieces):
+    starts, counts = [], []
+    start = 0
+    for i in range(pieces):
+        count = lax.shift_right_logical(lens_ref[i] + (LANES - 1), 7)
+        starts.append(start)
+        counts.append(count)
+        start = start + count
+    return starts, counts
+
+
+def pack_kernel(pieces, first, slots, by_column, lens_ref, pieces_ref, extra_ref, out_ref, stage, in_sems, out_sem):
+    starts, _ = block_starts(lens_ref, pieces)
+    blocks = pieces_ref.shape[1] // LANES
+    rows = slots * LANES
+    extra = stage.shape[1] - rows
+    chunk = GROUP // 4
+    for c in range(4):
+
+        @pl.loop(c * chunk, (c + 1) * chunk)
+        def _(d):
+            for q in range(slots):
+                slot = (first + q) * GROUP + d
+                piece, start = 0, 0
+                for i in range(1, pieces):
+                    after = slot >= starts[i]
+                    piece = jnp.where(after, i, piece)
+                    start = jnp.where(after, starts[i], start)
+                block = jnp.minimum(slot - start, blocks - 1)
+                pltpu.make_async_copy(
+                    pieces_ref.at[piece, pl.ds(pl.multiple_of(block * LANES, LANES), LANES), :],
+                    stage.at[d, pl.ds(q * LANES, LANES), :],
+                    in_sems.at[c],
+                ).start()
+            if by_column:
+                source = extra_ref.at[:, pl.ds(pl.multiple_of(d * LANES, LANES), LANES)]
+            else:
+                source = extra_ref
+            pltpu.make_async_copy(source, stage.at[d, pl.ds(rows, extra), :], in_sems.at[c]).start()
+
+    for c in range(4):
+        part = pl.ds(c * chunk, chunk)
+        pltpu.make_async_copy(out_ref.at[part], stage.at[part], in_sems.at[c]).wait()
+        pltpu.make_async_copy(stage.at[part], out_ref.at[part], out_sem.at[c]).start()
+    for c in range(4):
+        part = pl.ds(c * chunk, chunk)
+        pltpu.make_async_copy(stage.at[part], out_ref.at[part], out_sem.at[c]).wait()
+
+
+def pack(piece_lens, pieces, extra, first, slots, by_column):
+    rows = slots * LANES + extra.shape[0]
+    return pl.pallas_call(
+        functools.partial(pack_kernel, pieces.shape[0], first, slots, by_column),
+        out_shape=jax.ShapeDtypeStruct((GROUP, rows, LANES), jnp.bfloat16),
+        in_specs=[pl.BlockSpec(memory_space=pltpu.SMEM), hbm(), hbm()],
+        out_specs=pl.BlockSpec(memory_space=pltpu.HBM),
+        scratch_shapes=[
+            pltpu.VMEM((GROUP, rows, LANES), jnp.bfloat16),
+            pltpu.SemaphoreType.DMA((4,)),
+            pltpu.SemaphoreType.DMA((4,)),
+        ],
+        compiler_params=pltpu.CompilerParams(vmem_limit_bytes=24 << 20),
+        cost_estimate=pl.CostEstimate(flops=0, bytes_accessed=4 * GROUP * rows * LANES, transcendentals=0),
+        name="pack",
+    )(piece_lens, pieces, extra)
+
+
+def finish_kernel(pieces, tokens, scalars_ref, offset_ref, result_ref, attn_ref, value_ref):
+    starts, counts = block_starts(scalars_ref, pieces)
+    me = scalars_ref[pieces]
+    where = me * LANES + lax.broadcasted_iota(jnp.int32, (1, LANES), 1)
+    for i in range(pieces):
+        slot = jnp.minimum(starts[i] + jnp.minimum(me, counts[i]), pieces * GROUP - 1)
+        row = result_ref[slot & (GROUP - 1), pl.ds(tokens + lax.shift_right_logical(slot, 5), 1), :]
+        value_ref[i : i + 1, :] = jnp.where(where < scalars_ref[i], row + offset_ref[0], 0.0)
+    for s in range(GROUP):
+        attn_ref[:, s * LANES : (s + 1) * LANES] = result_ref[s, 0:tokens, :].astype(jnp.bfloat16)
+
+
+def finish(scalars, offset, result, pieces, tokens):
+    return pl.pallas_call(
+        functools.partial(finish_kernel, pieces, tokens),
+        out_shape=(
+            jax.ShapeDtypeStruct((tokens, GROUP * LANES), jnp.bfloat16),
+            jax.ShapeDtypeStruct((pieces, LANES), jnp.float32),
+        ),
+        in_specs=[pl.BlockSpec(memory_space=pltpu.SMEM)] * 2 + [vmem()],
+        out_specs=(vmem(), vmem()),
+        compiler_params=pltpu.CompilerParams(vmem_limit_bytes=16 << 20),
+        name="finish",
+    )(scalars, offset, result)
 
 
 def exchange(message):
@@ -221,7 +314,6 @@
     quarter = lax.dynamic_slice_in_dim(w_value, (core * 2 + yhi) * COLS, COLS, axis=1)
     w_own = lax.all_gather(quarter[None], ("x", "z", "yhi", "ylo"), axis=0, tiled=True)
     w_own = w_own.reshape(16, 2, 2 * LANES, COLS)
-    w_other = lax.ppermute(w_own, "core", [(0, 1), (1, 0)])
     order = jnp.stack([core, 1 - core])
     bias = b_value.reshape(2, 2, COLS)[order].reshape(4, COLS)
     score = w_score.reshape(2, 2, COLS)[order].reshape(4, COLS)
@@ -235,7 +327,7 @@
     cos = jnp.concatenate([jnp.cos(angles)] * 2, axis=-1)
     sin = jnp.concatenate([-jnp.sin(angles), jnp.sin(angles)], axis=-1)
     lens = jnp.broadcast_to(jnp.repeat(prompt_lens, steps)[:, None], (tokens, LANES))
-    heads = attention(
+    attend = lambda embedded: attention(
         embedded,
         attn_gain.astype(jnp.float32).reshape(GROUP, LANES),
         w_qkv,
@@ -247,30 +339,45 @@
     )
 
     pieces, length, _ = reward_pieces.shape
-    here = length // GROUP
-    blocks = reward_pieces.reshape(pieces, GROUP, here, LANES).transpose(1, 0, 2, 3)
-    split = pieces // 2
-    count = split * here
-    w_blocks = w_out.reshape(LANES, GROUP, LANES).transpose(1, 0, 2)
-    first = exchange(jnp.concatenate([blocks[:, :split].reshape(GROUP, count, LANES), w_blocks], axis=1))
-    second = exchange(
-        jnp.concatenate(
-            [
-                blocks[:, split:].reshape(GROUP, count, LANES),
-                jnp.broadcast_to(heads[None], (GROUP, tokens, LANES)),
-            ],
-            axis=1,
-        )
+    total = jnp.sum((piece_lens + (LANES - 1)) // LANES)
+    most = jnp.full((8, LANES), total, jnp.int32).astype(jnp.float32)
+    for axis in ("core", "yhi"):
+        most = jnp.maximum(most, lax.ppermute(most, axis, [(0, 1), (1, 0)]))
+    base = length // LANES * pieces // GROUP // 2
+    rest = jnp.clip((most[0, 0].astype(jnp.int32) + (GROUP - 1)) // GROUP - base, 0, base)
+
+    message = pack(piece_lens, reward_pieces, w_out, 0, base, True)
+    message, embedded = lax.optimization_barrier((message, embedded))
+    first = exchange(message)
+    heads = attend(embedded)
+    gain = reward_gain.astype(jnp.float32).reshape(GROUP, LANES)
+
+    def remainder(slots, first, heads, w_own, piece_lens, reward_pieces, gain, bias, score):
+        w_other = lax.ppermute(w_own, "core", [(0, 1), (1, 0)])
+        second = exchange(pack(piece_lens, reward_pieces, heads, base, slots, False))
+        parts = [score_rows(first, base, w_own, w_other, gain, bias, score)]
+        if slots:
+            parts.append(score_rows(second, slots, w_own, w_other, gain, bias, score))
+        if slots < base:
+            parts.append(jnp.zeros((base - slots, LANES), jnp.float32))
+        columns = project(first, base * LANES, second, slots * LANES, tokens)
+        return jnp.concatenate([columns] + parts, axis=0)
+
+    payload = lax.switch(
+        rest,
+        [functools.partial(remainder, slots) for slots in range(base + 1)],
+        first,
+        heads,
+        w_own,
+        piece_lens,
+        reward_pieces,
+        gain,
+        bias,
+        score,
     )
-    gain = reward_gain.astype(jnp.float32).reshape(GROUP, LANES)
-    scored = [score_rows(m, count, w_own, w_other, gain, bias, score) for m in (first, second)]
-    scored = jnp.concatenate([s.reshape(split, here) for s in scored], axis=0) + b_score[0]
-    where = me * here + jnp.arange(here, dtype=jnp.int32)
-    piece_values = jnp.where(where[None, :] < piece_lens[:, None], scored, 0.0)
-
-    columns = project(first, count, second, count, tokens)
-    attn_out = spread(columns).transpose(1, 0, 2).reshape(rows, steps, GROUP * LANES)
-    return (attn_out, piece_values)
+    scalars = jnp.concatenate([piece_lens, me.reshape(1).astype(jnp.int32)])
+    attn_out, piece_values = finish(scalars, b_score, spread(payload), pieces, tokens)
+    return (attn_out.reshape(rows, steps, GROUP * LANES), piece_values)
 
 
 def solution(mesh):

time: 293 us -> 256 us (0.87)
  waiting for transfers between devices: 163 us -> 137 us
  local copies, waits for them, and re-layouts: 40.2 us -> 20.6 us
  Pallas kernels: 30.4 us -> 45.6 us
  other arithmetic: 8.49 us -> 1.83 us
  starting transfers between devices: 35.1 us -> 32.1 us
    ppermute x1 -> x3, waiting for transfers between devices: 0.01 us -> 60 us  [the longest x2 60 us: per_device(): most = jnp.maximum(most, lax.ppermute(most, axis, [(0, 1), (1, 0)]))]
    all_gather x1, waiting for transfers between devices: 75.1 us -> 29.2 us  [per_device(): lax.all_gather(quarter[None], ('x', 'z', 'yhi', 'ylo'), axis=0, tiled=True)]
    all_to_all x4, waiting for transfers between devices: 87.6 us -> 48.3 us  [exchange(): return lax.all_to_all(message, MP, 0, 0)]
    pallas_call x2 -> x5, Pallas kernels: 27 us -> 41.4 us  [the longest x2 33.5 us: score_rows(): pl.pallas_call(functools.partial(score_kernel, slots), out_shape=jax.Shap...]
    reshape x5 -> x1, local copies, waits for them, and re-layouts: 11.8 us -> 0.8 us  [per_device(): return (attn_out.reshape(rows, steps, GROUP * LANES), piece_values)]
    concatenate x2, other arithmetic: 7.47 us -> 0.83 us  [the longest x1 0.76 us: remainder(): return jnp.concatenate([columns] + parts, axis=0)]
    all_to_all x4, starting transfers between devices: 35.1 us -> 29.1 us  [exchange(): return lax.all_to_all(message, MP, 0, 0)]
    slice x1, local copies, waits for them, and re-layouts: 6.26 us -> 0.51 us  [per_device(): most[0, 0].astype(jnp.int32) + (GROUP - 1)]
  transfers between devices with their start and end apart: 6 -> 8, of which waited for: 3 -> 6; matrix products, arithmetic and copies ran while one was open for 12% -> 4% of each run, Pallas kernels for 1% -> 4%
where the time goes in v2:
time: 256 us; the launch traced here: 254 us
  waiting for transfers between devices  137 us (54%)
  Pallas kernels  45.6 us (18%)
  starting transfers between devices  32.1 us (13%)
  local copies, waits for them, and re-layouts  20.6 us (8%)
  between operations  16.2 us (6%)
    ppermute x2, waiting for transfers between devices, per_device(): most = jnp.maximum(most, lax.ppermute(most, axis, [(0, 1), (1, 0)]))  60 us
    all_to_all x4, waiting for transfers between devices, exchange(): return lax.all_to_all(message, MP, 0, 0)  48.3 us
    pallas_call x2, Pallas kernels, score_rows(): pl.pallas_call(functools.partial(score_kernel, slots), out_shape=jax.Shap...  33.5 us
    all_gather x1, waiting for transfers between devices, per_device(): lax.all_gather(quarter[None], ('x', 'z', 'yhi', 'ylo'), axis=0, tiled=True)  29.2 us
    all_to_all x4, starting transfers between devices, exchange(): return lax.all_to_all(message, MP, 0, 0)  29.1 us
    unnamed x27, local copies, waits for them, and re-layouts  8.88 us
    pallas_call x2, Pallas kernels, pack(): pl.pallas_call(functools.partial(pack_kernel, pieces.shape[0], first, slo...  6.68 us
  transfers between devices with their start and end apart: 8, of which 6 were waited for; matrix products, arithmetic and copies ran while one was open for 4% of the time, Pallas kernels for 4%

profile of v2, /device:TPU:0, one launch (start us, length us, event | category | flops | bytes accessed | tf_op | source)
XLA Modules:
  0.0 254.1 jit_solution(4913047129667060433)
XLA Ops:
  7.2 1.0 copy-done
  8.2 0.7 constant_dynamic-slice_fusion
  8.9 0.8 copy.18
  9.8 5.0 %gather_fusion = bf16[32,128]{1,0:T(8,128)(2,1)S(1)} fusion(bf16[32000,128]{1,0:T(8,128)(2,1)} %param.22, s32[1024]{0:T(1024)S(1)} %pad_clamp_fusion.1), kind=kCustom, calls=%fused_computation | custom fusion | bytes 16512 | tf_op jit(solution)/shard_map/gather | solution.py:321
  14.7 0.7 broadcast_in_dim.11
  15.5 9.3 %all-to-all-start.5 = ((bf16[32,32,128]{2,1,0:T(8,128)(2,1)}), bf16[32,32,128]{2,1,0:T(8,128)(2,1)S(1)}, u32[]{:S(2)}, u32[]{:S(2)}) async-start(bf16[32,32,128]{2,1,0:T(8,128)(2,1)} %broadcast_in_dim.11), calls=%async_computation.5 | async-start | bytes 524288 | tf_op jit(solution)/shard_map/all_to_all | solution.py:284
  24.8 1.2 copy-done.11
  26.0 3.7 %pack.11 = bf16[32,640,128]{2,1,0:T(8,128)(2,1)S(1)} custom-call(s32[8]{0:T(128)} %lens_ref.1, bf16[8,4096,128]{2,1,0:T(8,128)(2,1)} %pieces_ref.1, bf16[128,4096]{1,0:T(8,128)(2,1)S(1)} %copy-done.11), custom_call_target="tpu_custom_call" | custom-call | bytes 10485760 | tf_op jit(solution)/shard_map/pack/pallas_call | solution.py:241
  29.7 2.4 copy-done.3
  32.2 2.4 all-to-all-done.5.emb_ref
  34.6 6.2 %all-to-all-start.6 = ((bf16[32,640,128]{2,1,0:T(8,128)(2,1)}), bf16[32,640,128]{2,1,0:T(8,128)(2,1)}, u32[]{:S(2)}, u32[]{:S(2)}) async-start(bf16[32,640,128]{2,1,0:T(8,128)(2,1)} %copy-done.3), calls=%async_computation.6 | async-start | bytes 10485760 | tf_op jit(solution)/shard_map/all_to_all | solution.py:284
  40.8 0.6 fusion.3
  43.3 2.9 %collective-permute-start.6 = (f32[8,128]{1,0:T(8,128)S(1)}, f32[8,128]{1,0:T(8,128)S(1)}, u32[]{:S(2)}, u32[]{:S(2)}) collective-permute-start(f32[8,128]{1,0:T(8,128)S(1)} %broadcast_maximum_fusion), channel_id=1, source_target_pairs={{0,64},{64,0},{1,65},{65,1},{2,66},{66,2},{3,67},{67,3},{4,68},{68... | collective-permute-start | bytes 12296 | tf_op jit(solution)/shard_map/ppermute | solution.py:345
  47.5 59.5 %collective-permute-done.6 = f32[8,128]{1,0:T(8,128)S(1)} collective-permute-done((f32[8,128]{1,0:T(8,128)S(1)}, f32[8,128]{1,0:T(8,128)S(1)}, u32[]{:S(2)}, u32[]{:S(2)}) %collective-permute-start.6) | collective-permute-done | bytes 4128 | tf_op jit(solution)/shard_map/ppermute | solution.py:345
  108.2 1.9 copy-done.8
  110.1 1.6 copy-done.10
  111.7 1.9 attention.1
  113.6 29.2 %all-gather.3.cloned.1.call-done = bf16[8192,512]{1,0:T(8,128)(2,1)} async-done(((bf16[128,512]{1,0:T(8,128)(2,1)}), bf16[8192,512]{1,0:T(8,128)(2,1)}) %all-gather.3.cloned.1.call-update) | async-done | bytes 8388624 | tf_op jit(solution)/shard_map/all_gather | solution.py:315
  142.8 81.1 %conditional.1 = (f32[40,128]{1,0:T(8,128)S(1)}) conditional(s32[]{:T(128)} %clamp.3, (s32[8]{0:T(128)S(1)}, bf16[8,4096,128]{2,1,0:T(8,128)(2,1)}, bf16[32,128]{1,0:T(8,128)(2,1)S(1)}, bf16[32,640,128]{2,1,0:T(8,128)(2,1)}, bf16[16,2,256,512]{3,2,1,0:T(8,128)(2,1)}, /*index=5*/f32[32,128]{1,0:T(8,128)S(1)}, ...), branch_computations={%region_1.2_spmd, %region_2.3_spmd, %region_3.4_spmd, %region_4.5_... | conditional | flops 17219878912 | bytes 121684064 | solution.py:366
  142.8 3.0 %pack.8 = bf16[32,288,128]{2,1,0:T(8,128)(2,1)S(1)} custom-call(s32[8]{0:T(128)S(1)} %get-tuple-element.103.lens_ref, bf16[8,4096,128]{2,1,0:T(8,128)(2,1)} %get-tuple-element.104.pieces_ref, bf16[32,128]{1,0:T(8,128)(2,1)S(1)} %get-tuple-element.105.extra_ref), custom_call_target="tpu_custom_call" | custom-call | bytes 4718592 | tf_op jit(solution)/shard_map/cond/branch_2_fun/pack/pallas_call | solution.py:241
  145.8 1.4 copy-done.7
  147.2 6.5 %all-to-all-start.2 = ((bf16[32,288,128]{2,1,0:T(8,128)(2,1)}), bf16[32,288,128]{2,1,0:T(8,128)(2,1)S(1)}, u32[]{:S(2)}, u32[]{:S(2)}) async-start(bf16[32,288,128]{2,1,0:T(8,128)(2,1)} %copy-done.7), calls=%async_computation.2 | async-start | bytes 4718592 | tf_op jit(solution)/shard_map/cond/branch_2_fun/all_to_all | solution.py:284
  153.7 33.2 %all-to-all-done.2.heads_ref.x_hbm = bf16[32,288,128]{2,1,0:T(8,128)(2,1)S(1)} async-done(((bf16[32,288,128]{2,1,0:T(8,128)(2,1)}), bf16[32,288,128]{2,1,0:T(8,128)(2,1)S(1)}, u32[]{:S(2)}, u32[]{:S(2)}) %all-to-all-start.2) | async-done | bytes 2359328 | tf_op jit(solution)/shard_map/cond/branch_2_fun/all_to_all | solution.py:284
  187.0 2.3 project.7
  189.3 13.6 %score.13 = f32[2,128]{1,0:T(2,128)} custom-call(bf16[32,288,128]{2,1,0:T(8,128)(2,1)} %copy-done.2, bf16[16,2,256,512]{3,2,1,0:T(8,128)(2,1)} %get-tuple-element.106.wa_hbm, bf16[16,2,256,512]{3,2,1,0:T(8,128)(2,1)} %collective-permute-done.2.wb_hbm, f32[32,128]{1,0:T(8,128)S(1)} %get-tuple-element.107.gain_ref, f32[4,512]{1,0:T(4,128)S(1)} %get-tuple-element.108.bias_ref, ...), custom_call_target="tpu_custom_call" | custom-call | flops 4294967296 | bytes 25165824 | tf_op jit(solution)/shard_map/cond/branch_2_fun/score/pallas_call | solution.py:169
  202.9 19.9 %score.12 = f32[4,128]{1,0:T(4,128)} custom-call(bf16[32,640,128]{2,1,0:T(8,128)(2,1)} %get-tuple-element.102.w_ref.x_hbm, bf16[16,2,256,512]{3,2,1,0:T(8,128)(2,1)} %get-tuple-element.106.wa_hbm, bf16[16,2,256,512]{3,2,1,0:T(8,128)(2,1)} %collective-permute-done.2.wb_hbm, f32[32,128]{1,0:T(8,128)S(1)} %get-tuple-element.107.gain_ref, ...), custom_call_target="tpu_custom_call" | custom-call | flops 8589934592 | bytes 25165824 | tf_op jit(solution)/shard_map/cond/branch_2_fun/score/pallas_call | solution.py:169
  222.9 0.8 maximum_maximum_fusion.2
  223.9 0.9 broadcast_in_dim.14
  224.8 7.1 %all-to-all-start.7 = ((f32[32,40,128]{2,1,0:T(8,128)}), f32[32,40,128]{2,1,0:T(8,128)S(1)}, u32[]{:S(2)}, u32[]{:S(2)}) async-start(f32[32,40,128]{2,1,0:T(8,128)} %broadcast_in_dim.14), calls=%async_computation.7 | async-start | bytes 1310720 | tf_op jit(solution)/shard_map/all_to_all | solution.py:284
  232.7 12.6 %all-to-all-done.7.result_ref = f32[32,40,128]{2,1,0:T(8,128)S(1)} async-done(((f32[32,40,128]{2,1,0:T(8,128)}), f32[32,40,128]{2,1,0:T(8,128)S(1)}, u32[]{:S(2)}, u32[]{:S(2)}) %all-to-all-start.7) | async-done | bytes 655392 | tf_op jit(solution)/shard_map/all_to_all | solution.py:284
  245.3 1.2 finish.1
  246.5 0.8 reshape.196
  (62 shorter events, 3.4 us)
Async XLA Ops:
  7.2 1.1 copy-start
  7.2 135.6 %all-gather.3.cloned.1.call-start = ((), (), s32[]{:S(2)}) async-start(), calls=%async_computation.8 | async-start | bytes 8519680 | tf_op jit(solution)/shard_map/all_gather | solution.py:315
  15.5 19.1 %all-to-all-start.5 = ((bf16[32,32,128]{2,1,0:T(8,128)(2,1)}), bf16[32,32,128]{2,1,0:T(8,128)(2,1)S(1)}, u32[]{:S(2)}, u32[]{:S(2)}) async-start(bf16[32,32,128]{2,1,0:T(8,128)(2,1)} %broadcast_in_dim.11), calls=%async_computation.5 | async-start | bytes 524288 | tf_op jit(solution)/shard_map/all_to_all | solution.py:284
  24.8 1.2 copy-start.11
  29.7 2.4 copy-start.3
  32.1 8.7 %copy-start.12 = (s32[8]{0:T(128)S(1)}, s32[8]{0:T(128)}, u32[]{:S(2)}) copy-start(s32[8]{0:T(128)} %lens_ref.1) | copy-start | bytes 100
  32.1 10.1 %copy-start.21 = (s32[8]{0:T(128)S(1)}, s32[8]{0:T(128)}, u32[]{:S(2)}) copy-start(s32[8]{0:T(128)} %param.21) | copy-start | bytes 100
  32.1 10.6 %copy-start.13 = (bf16[4096]{0:T(1024)(128)(2,1)S(1)}, bf16[4096]{0:T(1024)(128)(2,1)}, u32[]{:S(2)}) copy-start(bf16[4096]{0:T(1024)(128)(2,1)} %param.23) | copy-start | bytes 24580
  32.1 10.6 %copy-start.14 = (bf16[4096]{0:T(1024)(128)(2,1)S(1)}, bf16[4096]{0:T(1024)(128)(2,1)}, u32[]{:S(2)}) copy-start(bf16[4096]{0:T(1024)(128)(2,1)} %param.30) | copy-start | bytes 24580
  32.1 14.1 %copy-start.15 = (f32[2048]{0:T(1024)S(1)}, f32[2048]{0:T(1024)}, u32[]{:S(2)}) copy-start(f32[2048]{0:T(1024)} %param.32) | copy-start | bytes 24580
  32.1 14.7 %copy-start.16 = (f32[2048]{0:T(1024)S(1)}, f32[2048]{0:T(1024)}, u32[]{:S(2)}) copy-start(f32[2048]{0:T(1024)} %param.33) | copy-start | bytes 24580
  32.2 76.1 %copy-start.9 = (bf16[8,1,1024,128]{3,2,1,0:T(8,128)(2,1)S(1)}, bf16[8,1,1024,128]{3,2,1,0:T(8,128)(2,1)}, u32[]{:S(2)}) copy-start(bf16[8,1,1024,128]{3,2,1,0:T(8,128)(2,1)} %param.26) | copy-start | bytes 6291460
  34.6 79.0 %all-to-all-start.6 = ((bf16[32,640,128]{2,1,0:T(8,128)(2,1)}), bf16[32,640,128]{2,1,0:T(8,128)(2,1)}, u32[]{:S(2)}, u32[]{:S(2)}) async-start(bf16[32,640,128]{2,1,0:T(8,128)(2,1)} %copy-done.3), calls=%async_computation.6 | async-start | bytes 10485760 | tf_op jit(solution)/shard_map/all_to_all | solution.py:284
  42.1 1.2 collective-permute-start.5
  43.3 63.6 %collective-permute-start.6 = (f32[8,128]{1,0:T(8,128)S(1)}, f32[8,128]{1,0:T(8,128)S(1)}, u32[]{:S(2)}, u32[]{:S(2)}) collective-permute-start(f32[8,128]{1,0:T(8,128)S(1)} %broadcast_maximum_fusion), channel_id=1, source_target_pairs={{0,64},{64,0},{1,65},{65,1},{2,66},{66,2},{3,67},{67,3},{4,68},{68... | collective-permute-start | bytes 12296 | tf_op jit(solution)/shard_map/ppermute | solution.py:345
  108.2 1.9 copy-start.8
  110.1 1.6 copy-start.10
  142.8 46.5 %collective-permute-start.2 = (bf16[16,2,256,512]{3,2,1,0:T(8,128)(2,1)}, bf16[16,2,256,512]{3,2,1,0:T(8,128)(2,1)}, u32[]{:S(2)}, u32[]{:S(2)}) collective-permute-start(bf16[16,2,256,512]{3,2,1,0:T(8,128)(2,1)} %get-tuple-element.106.wa_hbm), channel_id=1, source_target_pairs={{0,32},{32,0},{1,33},{33,1},{2,34},{34,2},{3,35},{35,3},{4,36},{36... | collective-permute-start | bytes 25165832 | tf_op jit(solution)/shard_map/cond/branch_2_fun/ppermute | solution.py:356
  145.8 1.4 copy-start.7
  147.2 39.8 %all-to-all-start.2 = ((bf16[32,288,128]{2,1,0:T(8,128)(2,1)}), bf16[32,288,128]{2,1,0:T(8,128)(2,1)S(1)}, u32[]{:S(2)}, u32[]{:S(2)}) async-start(bf16[32,288,128]{2,1,0:T(8,128)(2,1)} %copy-done.7), calls=%async_computation.2 | async-start | bytes 4718592 | tf_op jit(solution)/shard_map/cond/branch_2_fun/all_to_all | solution.py:284
  187.0 2.3 copy-start.2
  202.9 20.0 %copy-start.17 = (f32[2,128]{1,0:T(2,128)S(1)}, f32[2,128]{1,0:T(2,128)}, u32[]{:S(2)}) copy-start(f32[2,128]{1,0:T(2,128)} %score.13) | copy-start | bytes 3076 | tf_op jit(solution)/shard_map/cond
  223.9 23.4 %copy-start.1 = (bf16[128,2048]{1,0:T(8,128)(2,1)S(1)}, bf16[128,2048]{1,0:T(8,128)(2,1)}, u32[]{:S(2)}) copy-start(bf16[128,2048]{1,0:T(8,128)(2,1)} %param.31) | copy-start | bytes 1572868
  224.8 20.5 %all-to-all-start.7 = ((f32[32,40,128]{2,1,0:T(8,128)}), f32[32,40,128]{2,1,0:T(8,128)S(1)}, u32[]{:S(2)}, u32[]{:S(2)}) async-start(f32[32,40,128]{2,1,0:T(8,128)} %broadcast_in_dim.14), calls=%async_computation.7 | async-start | bytes 1310720 | tf_op jit(solution)/shard_map/all_to_all | solution.py:284
Sparse Core Ops, SparseCore 0:
  10.9 131.8 all-gather.2
